TPU v7x, 32 devices: a whole 2x2x4 slice. The times are simulated.
32 devices in a mesh: grp: 2 (over y), seq: 16 (over z, x, core).
Axes of the slice: x: 2, y: 2, z: 4, core: 2. Of those that a mesh axis runs over, the one named last changes fastest.
Arguments:
- queries: bfloat16 [192, 8, 4096], P('seq', 'grp'), parts along dimension 1, may hold values from -7 to 7
- keys: bfloat16 [192, 8, 4096], P('seq', 'grp'), parts along dimension 1, may hold values from -7 to 7
- values: bfloat16 [192, 8, 4096], P('seq', 'grp'), parts along dimension 1, may hold values from -6 to 6
- clip_frames: int32 [8], P('grp'), parts along dimension 0, may hold values from 1 to 8, as said below
Outputs:
- attended: bfloat16 [192, 8, 4096], P('seq', 'grp'), parts along dimension 1
There are 2 independent parts, one for each index of `grp`. A program takes and returns all parts, laid end to end along the dimension named above; each array names one. Nothing has to cross between parts.
Inputs may be any that keep to these rules, and one draw needn't show every extreme that they name: Tokens of clip s at positions clip_frames[s] * 24 and later hold no data; some clip has all 8 frames.
All inputs are finite; a program needn't handle non-finite values.
Results may differ from a plain program's by a relative error of at most 0.0048.
Values may be sent and summed in bfloat16 or wider, within the bound.
A program may use at most 64 MiB of HBM per device.

v0:
```python
import functools
import math

import jax
import jax.numpy as jnp
from jax import lax
from jax.experimental import pallas as pl
from jax.experimental.pallas import tpu as pltpu
from jax.sharding import PartitionSpec as P

HEADS = 32
HDIM = 128
FRAMES = 8


neg_large = -1e30


def attend_block(query_block, key_rows, value_rows, key_bias):
    scores = jnp.einsum("qnd,knd->nqk", query_block, key_rows, preferred_element_type=jnp.float32)
    scores = scores * (1.0 / math.sqrt(HDIM)) + jnp.transpose(key_bias)[:, None, :]
    row_max = jnp.max(scores, axis=2, keepdims=True)
    exponent = jnp.exp(scores - row_max)
    weights = (exponent / jnp.sum(exponent, axis=2, keepdims=True)).astype(jnp.bfloat16)
    combined = jnp.einsum("nqk,knd->qnd", weights, value_rows, preferred_element_type=jnp.float32)
    return combined.astype(jnp.bfloat16)


def attend_all(query_rows, key_rows, value_rows, key_bias):
    length, item_count, head_dim = query_rows.shape
    block_rows = min(512, length)
    blocked = query_rows.reshape(length // block_rows, block_rows, item_count, head_dim)
    combined = lax.map(
        lambda query_block: attend_block(query_block, key_rows, value_rows, key_bias), blocked
    )
    return combined.reshape(length, item_count, head_dim)


def body(queries, keys, values, clip_frames):
    tokens, seq_count, feature_dim = queries.shape
    devices = lax.axis_size("seq")
    device_index = lax.axis_index("seq")
    slot_count = seq_count * HEADS
    per_device = slot_count // devices
    length = tokens * devices
    frame_tokens = length // FRAMES
    query_slots = queries.reshape(tokens, devices, per_device, HDIM)
    key_slots = keys.reshape(tokens, devices, per_device, HDIM)
    value_slots = values.reshape(tokens, devices, per_device, HDIM)
    slot_limit = jnp.repeat(clip_frames * frame_tokens, HEADS)
    query_all, key_all, value_all = (
        lax.all_to_all(query_slots, "seq", split_axis=1, concat_axis=0, tiled=True),
        lax.all_to_all(key_slots, "seq", split_axis=1, concat_axis=0, tiled=True),
        lax.all_to_all(value_slots, "seq", split_axis=1, concat_axis=0, tiled=True),
    )
    own_limit = lax.dynamic_slice_in_dim(slot_limit, device_index * per_device, per_device)
    key_place = jnp.arange(length, dtype=jnp.int32)
    key_bias = jnp.where(key_place[:, None] < own_limit[None, :], 0.0, neg_large).astype(
        jnp.float32
    )
    combined = attend_all(
        query_all.reshape(length, per_device, HDIM),
        key_all.reshape(length, per_device, HDIM),
        value_all.reshape(length, per_device, HDIM),
        key_bias,
    )
    combined = combined.reshape(length, 1, per_device, HDIM)
    returned = lax.all_to_all(combined, "seq", split_axis=0, concat_axis=1, tiled=True)
    return returned.reshape(tokens, seq_count, feature_dim)


def partner_of(me, step, count):
    place, other = 1, 0
    while place < count:
        other = other + ((me // place + (step // place) % 2) % 2) * place
        place *= 2
    return other


def fused(count, own_heads, frames_ref, q_ref, k_ref, v_ref, o_ref,
          held, wide, result, send_sem, recv_sem, osend_sem, orecv_sem, round_sem):
    tokens, clips, _ = q_ref.shape
    length = tokens * count
    me = lax.axis_index("seq")
    half = count // 2
    bits = [1 << bit for bit in range(half.bit_length())]
    order = sorted(range(1, count), key=lambda step: (step < half, step < half or step // 2 % 2 == 0))
    others = [partner_of(me, step, count) for step in order]
    sources = (k_ref, q_ref, v_ref)

    barrier = pltpu.get_barrier_semaphore()
    for bit in bits:
        pl.semaphore_signal(barrier, inc=1, device_id={"seq": partner_of(me, bit, count)})

    def columns(owner, head):
        return pl.ds(pl.multiple_of((owner * own_heads + head) * HDIM, HDIM), HDIM)

    own_rows = pl.ds(me * tokens, tokens)

    def send(head, steps):
        for step in steps:
            other = partner_of(me, step, count)
            for which, source in enumerate(sources):
                pltpu.make_async_remote_copy(
                    src_ref=source.at[:, :, columns(other, head)],
                    dst_ref=held.at[head, which, own_rows],
                    send_sem=send_sem.at[head, which],
                    recv_sem=recv_sem.at[head, which],
                    device_id={"seq": other},
                ).start()

    for head in range(own_heads):
        for which, source in enumerate(sources):
            pltpu.make_async_copy(
                source.at[:, :, columns(me, head)],
                held.at[head, which, own_rows],
                recv_sem.at[head, which],
            ).start()
    pl.semaphore_wait(barrier, len(bits))
    known = [0]
    ready = [half]
    for turn, bit in enumerate(reversed(bits[:-1])):
        pl.semaphore_signal(
            round_sem.at[turn], inc=1, device_id={"seq": partner_of(me, bit, count)}
        )
        send(0, ready)
        if turn == 0:
            for head in range(1, own_heads):
                send(head, ready)
        pl.semaphore_wait(round_sem.at[turn], 1)
        fresh = [low + bit for low in known]
        ready = [half + low for low in fresh]
        known = known + fresh
    send(0, ready)
    send(0, range(1, half))
    for head in range(1, own_heads):
        send(head, [step for step in order if step != half])

    place = lax.broadcasted_iota(jnp.int32, (length, length), 1)

    def arrived(head, which):
        whole = held.at[head, which]
        pltpu.make_async_copy(whole, whole, recv_sem.at[head, which]).wait()
        wide[which] = whole[...].astype(jnp.float32).reshape(length * clips, HDIM)

    def rows(which, clip):
        return wide[which, pl.ds(clip, length, stride=clips), :].astype(jnp.bfloat16)

    for head in range(own_heads):
        arrived(head, 0)
        arrived(head, 1)
        weights = []
        for clip in range(clips):
            scores = lax.dot_general(
                rows(1, clip), rows(0, clip), (((1,), (1,)), ((), ())),
                preferred_element_type=jnp.float32,
            ) * (1.0 / math.sqrt(HDIM))
            scores = jnp.where(place < frames_ref[clip] * (length // FRAMES), scores, -jnp.inf)
            exponent = jnp.exp(scores - jnp.max(scores, axis=1, keepdims=True))
            weights.append(
                (exponent / jnp.sum(exponent, axis=1, keepdims=True)).astype(jnp.bfloat16)
            )
        arrived(head, 2)
        for clip in range(clips):
            wide[3, pl.ds(clip, length, stride=clips), :] = jnp.dot(
                weights[clip], rows(2, clip), preferred_element_type=jnp.float32
            )
        result[head] = wide[3].reshape(length, clips, HDIM).astype(jnp.bfloat16)
        for other in others:
            pltpu.make_async_remote_copy(
                src_ref=result.at[head, pl.ds(other * tokens, tokens)],
                dst_ref=o_ref.at[:, :, columns(me, head)],
                send_sem=osend_sem.at[head],
                recv_sem=orecv_sem.at[0],
                device_id={"seq": other},
            ).start()
        pltpu.make_async_copy(
            result.at[head, own_rows], o_ref.at[:, :, columns(me, head)], orecv_sem.at[0]
        ).start()

    sent = held.at[0, 0, pl.ds(0, length - tokens)]
    for head in range(own_heads):
        for which in range(3):
            pltpu.make_async_copy(sent, sent, send_sem.at[head, which]).wait()
        pltpu.make_async_copy(sent, sent, osend_sem.at[head]).wait()
    pltpu.make_async_copy(o_ref, o_ref, orecv_sem.at[0]).wait()


def fused_body(queries, keys, values, clip_frames):
    tokens, clips, features = queries.shape
    count = lax.axis_size("seq")
    own_heads = HEADS // count
    length = tokens * count
    return pl.pallas_call(
        functools.partial(fused, count, own_heads),
        out_shape=pltpu.VMEM(queries.shape, jnp.bfloat16),
        in_specs=[pl.BlockSpec(memory_space=pltpu.SMEM)]
        + [pl.BlockSpec(memory_space=pl.ANY)] * 3,
        out_specs=pl.BlockSpec(memory_space=pltpu.VMEM),
        scratch_shapes=[
            pltpu.VMEM((own_heads, 3, length, clips, HDIM), jnp.bfloat16),
            pltpu.VMEM((4, length * clips, HDIM), jnp.float32),
            pltpu.VMEM((own_heads, length, clips, HDIM), jnp.bfloat16),
            pltpu.SemaphoreType.DMA((own_heads, 3)),
            pltpu.SemaphoreType.DMA((own_heads, 3)),
            pltpu.SemaphoreType.DMA((own_heads,)),
            pltpu.SemaphoreType.DMA((1,)),
            pltpu.SemaphoreType.REGULAR((max(count.bit_length() - 2, 1),)),
        ],
        compiler_params=pltpu.CompilerParams(collective_id=0, has_side_effects=True),
    )(clip_frames, queries, keys, values)


def solution(mesh):
    split_heads = mesh.shape["seq"] > 2 and HEADS % mesh.shape["seq"] == 0
    return jax.shard_map(
        fused_body if split_heads else body,
        mesh=mesh,
        in_specs=(P("seq", "grp", None), P("seq", "grp", None), P("seq", "grp", None), P("grp")),
        out_specs=P("seq", "grp", None),
        check_vma=False,
    )
```

profile of v0, /device:TPU:1, one launch (start us, length us, event | category | flops | bytes accessed | tf_op | source)
XLA Modules:
  0.0 40.9 jit_solution(6996155995207877209)
XLA Ops:
  0.0 40.1 %shard_map.46 = bf16[12,4,4096]{2,1,0:T(4,128)(2,1)S(1)} custom-call(s32[4]{0:T(128)} %frames_ref.1, bf16[12,4,4096]{2,1,0:T(4,128)(2,1)} %q_ref.1, bf16[12,4,4096]{2,1,0:T(4,128)(2,1)} %k_ref.1, bf16[12,4,4096]{2,1,0:T(4,128)(2,1)} %v_ref.1), custom_call_target="tpu_custom_call" | custom-call | tf_op jit(solution)/shard_map/pallas_call | solution.py:194
  40.1 0.7 %copy.6 = bf16[12,4,4096]{2,1,0:T(4,128)(2,1)} copy(bf16[12,4,4096]{2,1,0:T(4,128)(2,1)S(1)} %shard_map.46) | data formatting | bytes 786432
where the time goes:
time: 41.4 us; the launch traced here: 40.9 us
  Pallas kernels  40.1 us (97%)
  local copies, waits for them, and re-layouts  0.75 us (2%)
    pallas_call x1, Pallas kernels, fused_body(): pl.pallas_call(functools.partial(fused, count, own_heads), out_shape=pltp...  40.1 us

commit v1 on v0

--- a/solution.py
+++ b/solution.py
@@ -77,8 +77,8 @@
     return other
 
 
-def fused(count, own_heads, frames_ref, q_ref, k_ref, v_ref, o_ref,
-          held, wide, result, send_sem, recv_sem, osend_sem, orecv_sem, round_sem):
+def fused(count, own_heads, clip_ref, q_ref, k_ref, v_ref, o_ref,
+          held, wide, result, frames_ref, frames_sem, send_sem, recv_sem, osend_sem, orecv_sem, round_sem):
     tokens, clips, _ = q_ref.shape
     length = tokens * count
     me = lax.axis_index("seq")
@@ -109,13 +109,6 @@
                     device_id={"seq": other},
                 ).start()
 
-    for head in range(own_heads):
-        for which, source in enumerate(sources):
-            pltpu.make_async_copy(
-                source.at[:, :, columns(me, head)],
-                held.at[head, which, own_rows],
-                recv_sem.at[head, which],
-            ).start()
     pl.semaphore_wait(barrier, len(bits))
     known = [0]
     ready = [half]
@@ -136,7 +129,18 @@
     for head in range(1, own_heads):
         send(head, [step for step in order if step != half])
 
+    frames_copy = pltpu.make_async_copy(clip_ref, frames_ref, frames_sem.at[0])
+    frames_copy.start()
+    for head in range(own_heads):
+        for which, source in enumerate(sources):
+            pltpu.make_async_copy(
+                source.at[:, :, columns(me, head)],
+                held.at[head, which, own_rows],
+                recv_sem.at[head, which],
+            ).start()
     place = lax.broadcasted_iota(jnp.int32, (length, length), 1)
+
+    frames_copy.wait()
 
     def arrived(head, which):
         whole = held.at[head, which]
@@ -194,13 +198,14 @@
     return pl.pallas_call(
         functools.partial(fused, count, own_heads),
         out_shape=pltpu.VMEM(queries.shape, jnp.bfloat16),
-        in_specs=[pl.BlockSpec(memory_space=pltpu.SMEM)]
-        + [pl.BlockSpec(memory_space=pl.ANY)] * 3,
+        in_specs=[pl.BlockSpec(memory_space=pl.ANY)] * 4,
         out_specs=pl.BlockSpec(memory_space=pltpu.VMEM),
         scratch_shapes=[
             pltpu.VMEM((own_heads, 3, length, clips, HDIM), jnp.bfloat16),
             pltpu.VMEM((4, length * clips, HDIM), jnp.float32),
             pltpu.VMEM((own_heads, length, clips, HDIM), jnp.bfloat16),
+            pltpu.SMEM(clip_frames.shape, jnp.int32),
+            pltpu.SemaphoreType.DMA((1,)),
             pltpu.SemaphoreType.DMA((own_heads, 3)),
             pltpu.SemaphoreType.DMA((own_heads, 3)),
             pltpu.SemaphoreType.DMA((own_heads,)),

time: 41.4 us -> 40.7 us (0.983)
  Pallas kernels: 40.1 us -> 39.4 us
    pallas_call x1, Pallas kernels: 40.1 us -> 39.4 us  [fused_body(): pl.pallas_call(functools.partial(fused, count, own_heads), out_shape=pltp...]
where the time goes in v1:
time: 40.7 us; the launch traced here: 40.1 us
  Pallas kernels  39.4 us (97%)
  local copies, waits for them, and re-layouts  0.75 us (2%)
    pallas_call x1, Pallas kernels, fused_body(): pl.pallas_call(functools.partial(fused, count, own_heads), out_shape=pltp...  39.4 us

profile of v1, /device:TPU:1, one launch (start us, length us, event | category | flops | bytes accessed | tf_op | source)
XLA Modules:
  0.0 40.1 jit_solution(6610603581904562675)
XLA Ops:
  0.0 39.4 %shard_map.46 = bf16[12,4,4096]{2,1,0:T(4,128)(2,1)S(1)} custom-call(s32[4]{0:T(128)} %clip_ref.1, bf16[12,4,4096]{2,1,0:T(4,128)(2,1)} %q_ref.1, bf16[12,4,4096]{2,1,0:T(4,128)(2,1)} %k_ref.1, bf16[12,4,4096]{2,1,0:T(4,128)(2,1)} %v_ref.1), custom_call_target="tpu_custom_call" | custom-call | tf_op jit(solution)/shard_map/pallas_call | solution.py:198
  39.4 0.7 %copy.6 = bf16[12,4,4096]{2,1,0:T(4,128)(2,1)} copy(bf16[12,4,4096]{2,1,0:T(4,128)(2,1)S(1)} %shard_map.46) | data formatting | bytes 786432

commit v2 on v1

--- a/solution.py
+++ b/solution.py
@@ -11,6 +11,14 @@
 HEADS = 32
 HDIM = 128
 FRAMES = 8
+
+OPENING = ('b', 'c', 'c', 'b')
+ORDERS = {
+    'first': ('anc', 'abn', 'anb', 'cna'),
+    'later': ('bnac', 'bcna', 'cban', 'cban'),
+    'return': ('bcan', 'bcan', 'bcan', 'bcan'),
+    'last': ('canb', 'bcan', 'bcan', 'canb'),
+}
 
 
 neg_large = -1e30
@@ -69,38 +77,54 @@
     return returned.reshape(tokens, seq_count, feature_dim)
 
 
-def partner_of(me, step, count):
-    place, other = 1, 0
-    while place < count:
-        other = other + ((me // place + (step // place) % 2) % 2) * place
-        place *= 2
-    return other
-
-
 def fused(count, own_heads, clip_ref, q_ref, k_ref, v_ref, o_ref,
-          held, wide, result, frames_ref, frames_sem, send_sem, recv_sem, osend_sem, orecv_sem, round_sem):
+          held, wide, result, frames_ref, frames_sem, send_sem, recv_sem, osend_sem, orecv_sem, round_sem, reply_sem):
     tokens, clips, _ = q_ref.shape
     length = tokens * count
     me = lax.axis_index("seq")
-    half = count // 2
-    bits = [1 << bit for bit in range(half.bit_length())]
-    order = sorted(range(1, count), key=lambda step: (step < half, step < half or step // 2 % 2 == 0))
-    others = [partner_of(me, step, count) for step in order]
+    quarter = count // 4
+    layer = me // quarter
+    last = layer // 3
+    flips = [(1 - 2 * (me // (1 << bit) % 2)) * (1 << bit) for bit in range(count.bit_length() - 1)]
+    mates = range(quarter.bit_length() - 1)
+    lows = sorted(range(quarter), key=lambda low: low // 2 % 2 == 0)
     sources = (k_ref, q_ref, v_ref)
 
+    def flipped(mask):
+        return sum(flip for bit, flip in enumerate(flips) if mask >> bit & 1)
+
+    leads = {"n": 0, "a": quarter, "b": 2 * quarter, "c": 3 * quarter}
+
+    def pick(masks):
+        value = flipped(masks[3])
+        for index in range(3):
+            if masks[index] != masks[3]:
+                value = jnp.where(layer == index, flipped(masks[index]), value)
+        return me + value
+
+    def sequence(words):
+        plans = [[leads[block] + low for block in word for low in lows] for word in words]
+        return [pick(masks) for masks in zip(*[[mask for mask in plan if mask] for plan in plans])]
+
     barrier = pltpu.get_barrier_semaphore()
-    for bit in bits:
-        pl.semaphore_signal(barrier, inc=1, device_id={"seq": partner_of(me, bit, count)})
+    for bit in mates:
+        pl.semaphore_signal(barrier, inc=1, device_id={"seq": me + flips[bit]})
+
+    @pl.when(last == 0)
+    def _():
+        for block in "abc":
+            pl.semaphore_signal(barrier, inc=1, device_id={"seq": me + flipped(leads[block])})
+
+    opening = [pick([leads[block] + low for block in OPENING]) for low in range(quarter)]
 
     def columns(owner, head):
         return pl.ds(pl.multiple_of((owner * own_heads + head) * HDIM, HDIM), HDIM)
 
     own_rows = pl.ds(me * tokens, tokens)
 
-    def send(head, steps):
-        for step in steps:
-            other = partner_of(me, step, count)
-            for which, source in enumerate(sources):
+    def send(head, others):
+        for which, source in enumerate(sources):
+            for other in others:
                 pltpu.make_async_remote_copy(
                     src_ref=source.at[:, :, columns(other, head)],
                     dst_ref=held.at[head, which, own_rows],
@@ -109,25 +133,29 @@
                     device_id={"seq": other},
                 ).start()
 
-    pl.semaphore_wait(barrier, len(bits))
-    known = [0]
-    ready = [half]
-    for turn, bit in enumerate(reversed(bits[:-1])):
-        pl.semaphore_signal(
-            round_sem.at[turn], inc=1, device_id={"seq": partner_of(me, bit, count)}
-        )
-        send(0, ready)
-        if turn == 0:
-            for head in range(1, own_heads):
-                send(head, ready)
-        pl.semaphore_wait(round_sem.at[turn], 1)
-        fresh = [low + bit for low in known]
-        ready = [half + low for low in fresh]
-        known = known + fresh
-    send(0, ready)
-    send(0, range(1, half))
+    pl.semaphore_wait(barrier, len(mates) + 2 + last)
+
+    @pl.when(last == 1)
+    def _():
+        for block in "abc":
+            pl.semaphore_signal(reply_sem.at[0], inc=1, device_id={"seq": me + flipped(leads[block])})
+
+    send(0, opening[:1])
+    for bit in mates:
+        pl.semaphore_signal(round_sem.at[0, bit], inc=1, device_id={"seq": me + flips[bit]})
+        pl.semaphore_wait(round_sem.at[0, bit], 1)
+        send(0, opening[1 << bit : 2 << bit])
+
+    @pl.when(last == 0)
+    def _():
+        pl.semaphore_wait(reply_sem.at[0], 1)
+
+    for bit in mates:
+        pl.semaphore_signal(round_sem.at[1, bit], inc=1, device_id={"seq": me + flips[bit]})
+        pl.semaphore_wait(round_sem.at[1, bit], 1)
+    send(0, sequence(ORDERS["first"]))
     for head in range(1, own_heads):
-        send(head, [step for step in order if step != half])
+        send(head, sequence(ORDERS["later"]))
 
     frames_copy = pltpu.make_async_copy(clip_ref, frames_ref, frames_sem.at[0])
     frames_copy.start()
@@ -170,7 +198,7 @@
                 weights[clip], rows(2, clip), preferred_element_type=jnp.float32
             )
         result[head] = wide[3].reshape(length, clips, HDIM).astype(jnp.bfloat16)
-        for other in others:
+        for other in sequence(ORDERS["return" if head + 1 < own_heads else "last"]):
             pltpu.make_async_remote_copy(
                 src_ref=result.at[head, pl.ds(other * tokens, tokens)],
                 dst_ref=o_ref.at[:, :, columns(me, head)],
@@ -210,14 +238,15 @@
             pltpu.SemaphoreType.DMA((own_heads, 3)),
             pltpu.SemaphoreType.DMA((own_heads,)),
             pltpu.SemaphoreType.DMA((1,)),
-            pltpu.SemaphoreType.REGULAR((max(count.bit_length() - 2, 1),)),
+            pltpu.SemaphoreType.REGULAR((2, count.bit_length())),
+            pltpu.SemaphoreType.REGULAR((1,)),
         ],
         compiler_params=pltpu.CompilerParams(collective_id=0, has_side_effects=True),
     )(clip_frames, queries, keys, values)
 
 
 def solution(mesh):
-    split_heads = mesh.shape["seq"] > 2 and HEADS % mesh.shape["seq"] == 0
+    split_heads = mesh.shape["seq"] >= 8 and HEADS % mesh.shape["seq"] == 0
     return jax.shard_map(
         fused_body if split_heads else body,
         mesh=mesh,

time: 40.7 us -> 40.1 us (0.985)
  no operation moved by 1% of the time
where the time goes in v2:
time: 40.1 us; the launch traced here: 39.9 us
  Pallas kernels  39.2 us (98%)
  local copies, waits for them, and re-layouts  0.75 us (2%)
    pallas_call x1, Pallas kernels, fused_body(): pl.pallas_call(functools.partial(fused, count, own_heads), out_shape=pltp...  39.2 us

profile of v2, /device:TPU:1, one launch (start us, length us, event | category | flops | bytes accessed | tf_op | source)
XLA Modules:
  0.0 39.9 jit_solution(12678064437162062786)
XLA Ops:
  0.0 39.2 %shard_map.46 = bf16[12,4,4096]{2,1,0:T(4,128)(2,1)S(1)} custom-call(s32[4]{0:T(128)} %clip_ref.1, bf16[12,4,4096]{2,1,0:T(4,128)(2,1)} %q_ref.1, bf16[12,4,4096]{2,1,0:T(4,128)(2,1)} %k_ref.1, bf16[12,4,4096]{2,1,0:T(4,128)(2,1)} %v_ref.1), custom_call_target="tpu_custom_call" | custom-call | tf_op jit(solution)/shard_map/pallas_call | solution.py:226
  39.2 0.7 %copy.6 = bf16[12,4,4096]{2,1,0:T(4,128)(2,1)} copy(bf16[12,4,4096]{2,1,0:T(4,128)(2,1)S(1)} %shard_map.46) | data formatting | bytes 786432

commit v3 on v2

--- a/solution.py
+++ b/solution.py
@@ -78,7 +78,7 @@
 
 
 def fused(count, own_heads, clip_ref, q_ref, k_ref, v_ref, o_ref,
-          held, wide, result, frames_ref, frames_sem, send_sem, recv_sem, osend_sem, orecv_sem, round_sem, reply_sem):
+          held, wide, result, staged, staged_sem, frames_ref, frames_sem, send_sem, recv_sem, osend_sem, orecv_sem, round_sem, reply_sem):
     tokens, clips, _ = q_ref.shape
     length = tokens * count
     me = lax.axis_index("seq")
@@ -106,6 +106,12 @@
         plans = [[leads[block] + low for block in word for low in lows] for word in words]
         return [pick(masks) for masks in zip(*[[mask for mask in plan if mask] for plan in plans])]
 
+    loads = [
+        pltpu.make_async_copy(source, staged.at[which], staged_sem.at[which])
+        for which, source in enumerate(sources)
+    ]
+    for load in loads:
+        load.start()
     barrier = pltpu.get_barrier_semaphore()
     for bit in mates:
         pl.semaphore_signal(barrier, inc=1, device_id={"seq": me + flips[bit]})
@@ -123,10 +129,10 @@
     own_rows = pl.ds(me * tokens, tokens)
 
     def send(head, others):
-        for which, source in enumerate(sources):
+        for which in range(3):
             for other in others:
                 pltpu.make_async_remote_copy(
-                    src_ref=source.at[:, :, columns(other, head)],
+                    src_ref=staged.at[which, :, :, columns(other, head)],
                     dst_ref=held.at[head, which, own_rows],
                     send_sem=send_sem.at[head, which],
                     recv_sem=recv_sem.at[head, which],
@@ -140,6 +146,8 @@
         for block in "abc":
             pl.semaphore_signal(reply_sem.at[0], inc=1, device_id={"seq": me + flipped(leads[block])})
 
+    for load in loads:
+        load.wait()
     send(0, opening[:1])
     for bit in mates:
         pl.semaphore_signal(round_sem.at[0, bit], inc=1, device_id={"seq": me + flips[bit]})
@@ -232,6 +240,8 @@
             pltpu.VMEM((own_heads, 3, length, clips, HDIM), jnp.bfloat16),
             pltpu.VMEM((4, length * clips, HDIM), jnp.float32),
             pltpu.VMEM((own_heads, length, clips, HDIM), jnp.bfloat16),
+            pltpu.VMEM((3,) + queries.shape, jnp.bfloat16),
+            pltpu.SemaphoreType.DMA((3,)),
             pltpu.SMEM(clip_frames.shape, jnp.int32),
             pltpu.SemaphoreType.DMA((1,)),
             pltpu.SemaphoreType.DMA((own_heads, 3)),

time: 40.1 us -> 39.8 us (level)
  no operation moved by 1% of the time
where the time goes in v3:
time: 39.8 us; the launch traced here: 39.7 us
  Pallas kernels  38.9 us (98%)
  local copies, waits for them, and re-layouts  0.75 us (2%)
    pallas_call x1, Pallas kernels, fused_body(): pl.pallas_call(functools.partial(fused, count, own_heads), out_shape=pltp...  38.9 us

profile of v3, /device:TPU:1, one launch (start us, length us, event | category | flops | bytes accessed | tf_op | source)
XLA Modules:
  0.0 39.7 jit_solution(12594705416222068631)
XLA Ops:
  0.0 38.9 %shard_map.46 = bf16[12,4,4096]{2,1,0:T(4,128)(2,1)S(1)} custom-call(s32[4]{0:T(128)} %clip_ref.1, bf16[12,4,4096]{2,1,0:T(4,128)(2,1)} %q_ref.1, bf16[12,4,4096]{2,1,0:T(4,128)(2,1)} %k_ref.1, bf16[12,4,4096]{2,1,0:T(4,128)(2,1)} %v_ref.1), custom_call_target="tpu_custom_call" | custom-call | tf_op jit(solution)/shard_map/pallas_call | solution.py:234
  38.9 0.7 %copy.6 = bf16[12,4,4096]{2,1,0:T(4,128)(2,1)} copy(bf16[12,4,4096]{2,1,0:T(4,128)(2,1)S(1)} %shard_map.46) | data formatting | bytes 786432

commit v4 on v3

--- a/solution.py
+++ b/solution.py
@@ -128,8 +128,10 @@
 
     own_rows = pl.ds(me * tokens, tokens)
 
-    def send(head, others):
+    def send(head, others, loads=()):
         for which in range(3):
+            for load in loads[which : which + 1]:
+                load.wait()
             for other in others:
                 pltpu.make_async_remote_copy(
                     src_ref=staged.at[which, :, :, columns(other, head)],
@@ -146,9 +148,7 @@
         for block in "abc":
             pl.semaphore_signal(reply_sem.at[0], inc=1, device_id={"seq": me + flipped(leads[block])})
 
-    for load in loads:
-        load.wait()
-    send(0, opening[:1])
+    send(0, opening[:1], loads)
     for bit in mates:
         pl.semaphore_signal(round_sem.at[0, bit], inc=1, device_id={"seq": me + flips[bit]})
         pl.semaphore_wait(round_sem.at[0, bit], 1)

time: 39.8 us -> 39.8 us (level)
  no operation moved by 1% of the time
where the time goes in v4:
time: 39.8 us; the launch traced here: 39.7 us
  Pallas kernels  38.9 us (98%)
  local copies, waits for them, and re-layouts  0.75 us (2%)
    pallas_call x1, Pallas kernels, fused_body(): pl.pallas_call(functools.partial(fused, count, own_heads), out_shape=pltp...  38.9 us

profile of v4, /device:TPU:1, one launch (start us, length us, event | category | flops | bytes accessed | tf_op | source)
XLA Modules:
  0.0 39.7 jit_solution(8916728181444220010)
XLA Ops:
  0.0 38.9 %shard_map.46 = bf16[12,4,4096]{2,1,0:T(4,128)(2,1)S(1)} custom-call(s32[4]{0:T(128)} %clip_ref.1, bf16[12,4,4096]{2,1,0:T(4,128)(2,1)} %q_ref.1, bf16[12,4,4096]{2,1,0:T(4,128)(2,1)} %k_ref.1, bf16[12,4,4096]{2,1,0:T(4,128)(2,1)} %v_ref.1), custom_call_target="tpu_custom_call" | custom-call | tf_op jit(solution)/shard_map/pallas_call | solution.py:234
  38.9 0.7 %copy.6 = bf16[12,4,4096]{2,1,0:T(4,128)(2,1)} copy(bf16[12,4,4096]{2,1,0:T(4,128)(2,1)S(1)} %shard_map.46) | data formatting | bytes 786432

commit v5 on v4

--- a/solution.py
+++ b/solution.py
@@ -170,7 +170,7 @@
     for head in range(own_heads):
         for which, source in enumerate(sources):
             pltpu.make_async_copy(
-                source.at[:, :, columns(me, head)],
+                staged.at[which, :, :, columns(me, head)],
                 held.at[head, which, own_rows],
                 recv_sem.at[head, which],
             ).start()

time: 39.8 us -> 39.8 us (level)
  no operation moved by 1% of the time
where the time goes in v5:
time: 39.8 us; the launch traced here: 39.7 us
  Pallas kernels  38.9 us (98%)
  local copies, waits for them, and re-layouts  0.75 us (2%)
    pallas_call x1, Pallas kernels, fused_body(): pl.pallas_call(functools.partial(fused, count, own_heads), out_shape=pltp...  38.9 us

profile of v5, /device:TPU:1, one launch (start us, length us, event | category | flops | bytes accessed | tf_op | source)
XLA Modules:
  0.0 39.7 jit_solution(3436881300048128575)
XLA Ops:
  0.0 38.9 %shard_map.46 = bf16[12,4,4096]{2,1,0:T(4,128)(2,1)S(1)} custom-call(s32[4]{0:T(128)} %clip_ref.1, bf16[12,4,4096]{2,1,0:T(4,128)(2,1)} %q_ref.1, bf16[12,4,4096]{2,1,0:T(4,128)(2,1)} %k_ref.1, bf16[12,4,4096]{2,1,0:T(4,128)(2,1)} %v_ref.1), custom_call_target="tpu_custom_call" | custom-call | tf_op jit(solution)/shard_map/pallas_call | solution.py:234
  38.9 0.7 %copy.6 = bf16[12,4,4096]{2,1,0:T(4,128)(2,1)} copy(bf16[12,4,4096]{2,1,0:T(4,128)(2,1)S(1)} %shard_map.46) | data formatting | bytes 786432
